TPU v7x, 512 devices: a whole 4x8x8 slice. The times are simulated.
512 devices in a mesh: ctx: 64 (over y, z), tp: 8 (over x, core).
Axes of the slice: x: 4, y: 8, z: 8, core: 2. Of those that a mesh axis runs over, the one named last changes fastest.
Arguments:
- query: bfloat16 [8192, 8192], P('ctx', 'tp'), may hold values from -6 to 6
- keyed: bfloat16 [8192, 8192], P('ctx', 'tp'), may hold values from -6 to 6
- valued: bfloat16 [8192, 8192], P('ctx', 'tp'), may hold values from -6 to 6
- short_taps: float32 [3, 3, 8192], P(None, None, 'tp'), may hold values from -3.5 to 3.5
- rates: float32 [8, 8192], P(None, 'tp'), may hold values from 3.0517578e-05 to 0.1
- residues: float32 [8, 8192], P(None, 'tp'), may hold values from -1.5 to 1.5
- skip_gain: float32 [8192], P('tp'), may hold values from -1.6 to 1.6
- doc_ids: int32 [8192], P('ctx'), may hold values from 0 to 7, never falling along the last dimension, each value on 1 to 4096 neighbouring positions
Outputs:
- mixed: bfloat16 [8192, 8192], P('ctx', 'tp')
Inputs may be any that keep to these rules, and one draw needn't show every extreme that they name: doc_ids never falls along the sequence; each of the 8 documents holds 1 to 4096 consecutive tokens, one exactly 4096.
All inputs are finite; a program needn't handle non-finite values.
Results may differ from a plain program's by a relative error of at most 0.0065.
Values may be sent and summed in bfloat16 or wider, within the bound.
A program may use at most 128 MiB of HBM per device.

v0:
```python
import jax
import jax.numpy as jnp
from jax import lax
from jax.sharding import PartitionSpec as P


def shifted_2(value, axis, steps):
    count = lax.axis_size(axis)
    first, last = (max(0, -steps), min(count, count - steps))
    return lax.ppermute(value, axis, [(source, source + steps) for source in range(first, last)])


def short_conv(ext, ids_ext, taps):
    width = taps.shape[1] - 1
    length = ext.shape[1] - width
    total = jnp.zeros((ext.shape[0], length, ext.shape[2]), jnp.float32)
    for tap in range(taps.shape[1]):
        seg = ext[:, width - tap : width - tap + length]
        same = (ids_ext[width - tap : width - tap + length] == ids_ext[width:]).astype(jnp.float32)
        total = total + taps[:, tap][:, None, :] * seg * same[None, :, None]
    return total


def mode_terms_all(gated, ids, rates, residues):
    block, channels = gated.shape
    order = rates.shape[0]
    places = jnp.arange(block, dtype=jnp.float32)
    shifted = places - float(block // 2)
    lower = places[:, None] >= places[None, :]
    mask = (lower & (ids[:, None] == ids[None, :])).astype(jnp.float32)
    grow = jnp.exp(rates[None] * shifted[:, None, None])
    weighted = (grow * gated[:, None, :]).reshape(block, order * channels)
    summed = jnp.dot(mask, weighted, precision=lax.Precision.HIGHEST).reshape(
        block, order, channels
    )
    states = summed * jnp.exp(-rates[None] * shifted[:, None, None])
    long_part = jnp.sum(residues[None] * states, axis=1)
    return (long_part, states[block - 1])


def incoming(carry, ids, prev_last, rates, residues):
    block = ids.shape[0]
    places = jnp.arange(block, dtype=jnp.float32) + 1.0
    live = (ids == prev_last).astype(jnp.float32)
    total = jnp.zeros((block, rates.shape[1]), jnp.float32)
    for group in range(rates.shape[0] // 4):
        rate = rates[4 * group : 4 * group + 4]
        weight = residues[4 * group : 4 * group + 4] * carry[4 * group : 4 * group + 4]
        total = total + jnp.sum(weight[None] * jnp.exp(-rate[None] * places[:, None, None]), axis=1)
    return total * live[:, None]


def transition(ids, prev_last, rates):
    block = ids.shape[0]
    keep = ((ids[0] == prev_last) & (ids[0] == ids[block - 1])).astype(jnp.float32)
    return jnp.exp(-rates * block) * keep


def combine(earlier, later):
    return (earlier[0] * later[0], later[0] * earlier[1] + later[1])


def on_device(query, keyed, valued, short_taps, rates, residues, skip_gain, doc_ids):
    block, channels = query.shape
    width = short_taps.shape[1] - 1
    stacked = jnp.stack([query, keyed, valued])
    prev_rows, prev_ids = shifted_2(
        (stacked[:, block - width :], doc_ids[block - width :]), "ctx", 1
    )
    ext = jnp.concatenate([prev_rows, stacked], axis=1).astype(jnp.float32)
    ids_ext = jnp.concatenate([prev_ids, doc_ids])
    conv = short_conv(ext, ids_ext, short_taps)
    gated = (conv[1] * conv[2]).astype(jnp.bfloat16)
    gated_f = gated.astype(jnp.float32)
    n_ctx = lax.axis_size("ctx")
    group_width = channels // n_ctx
    whole = lax.all_to_all(gated, "ctx", split_axis=1, concat_axis=0, tiled=True)
    ids_all = lax.all_gather(doc_ids, "ctx", axis=0, tiled=True)
    offset = lax.axis_index("ctx") * group_width
    rate_sub = lax.dynamic_slice_in_dim(rates, offset, group_width, 1)
    resid_sub = lax.dynamic_slice_in_dim(residues, offset, group_width, 1)
    blocks_u = whole.reshape(n_ctx, block, group_width).astype(jnp.float32)
    blocks_ids = ids_all.reshape(n_ctx, block)
    prev_lasts = jnp.concatenate([jnp.zeros((1,), jnp.int32), blocks_ids[:-1, block - 1]])
    local_parts, ends = jax.vmap(lambda uu, ii: mode_terms_all(uu, ii, rate_sub, resid_sub))(
        blocks_u, blocks_ids
    )
    keeps = jax.vmap(lambda ii, pp: transition(ii, pp, rate_sub))(blocks_ids, prev_lasts)
    _, inclusive = lax.associative_scan(combine, (keeps, ends), axis=0)
    carries = jnp.concatenate([jnp.zeros_like(inclusive[:1]), inclusive[:-1]], axis=0)
    entering = jax.vmap(lambda cc, ii, pp: incoming(cc, ii, pp, rate_sub, resid_sub))(
        carries, blocks_ids, prev_lasts
    )
    grouped = (local_parts + entering).reshape(n_ctx * block, group_width)
    long_all = lax.all_to_all(grouped, "ctx", split_axis=0, concat_axis=1, tiled=True)
    return (conv[0] * (long_all + skip_gain[None] * gated_f)).astype(jnp.bfloat16)


def solution(mesh):
    return jax.shard_map(
        on_device,
        mesh=mesh,
        in_specs=(
            P("ctx", "tp"),
            P("ctx", "tp"),
            P("ctx", "tp"),
            P(None, None, "tp"),
            P(None, "tp"),
            P(None, "tp"),
            P("tp"),
            P("ctx"),
        ),
        out_specs=P("ctx", "tp"),
        check_vma=False,
    )
```

profile of v0, /device:TPU:4, one launch (start us, length us, event | category | flops | bytes accessed | tf_op | source)
XLA Modules:
  0.0 192.9 jit_solution(2154041682382078537)
XLA Ops:
  0.0 1.1 copy.45
  1.2 1.1 copy.44
  2.3 1.1 copy.43
  3.4 0.3 pad_maximum_fusion
  3.7 0.3 copy.46
  4.0 4.3 %collective-permute-start = (bf16[3,2,1024]{2,1,0:T(2,128)(2,1)S(1)}, bf16[3,2,1024]{2,1,0:T(2,128)(2,1)S(1)}, u32[]{:S(2)}, u32[]{:S(2)}) collective-permute-start(bf16[3,2,1024]{2,1,0:T(2,128)(2,1)S(1)} %copy.46), channel_id=1, source_target_pairs={{0,8},{8,16},{16,24},{24,32},{32,40},{40,48},{48,56},{56,64},{64,7... | collective-permute-start | bytes 36872 | tf_op jit(solution)/shard_map/ppermute | solution.py:10
  8.3 0.1 slice.217
  8.4 4.3 %collective-permute-start.1 = (s32[2]{0:T(128)S(1)}, s32[2]{0:T(128)S(1)}, u32[]{:S(2)}, u32[]{:S(2)}) collective-permute-start(s32[2]{0:T(128)S(1)} %slice.217), channel_id=1, source_target_pairs={{0,8},{8,16},{16,24},{24,32},{32,40},{40,48},{48,56},{56,64},{64,7... | collective-permute-start | bytes 32 | tf_op jit(solution)/shard_map/ppermute | solution.py:10
  12.7 0.8 multiply_exponential_fusion.4
  13.4 0.1 mul.302
  13.5 47.9 %all-gather = s32[64,1,128]{2,1,0:T(1,128)S(1)} all-gather(s32[1,1,128]{2,1,0:T(1,128)S(1)} %bitcast.48), channel_id=1, replica_groups=mesh['ctx'=64,'tp'=8] {'ctx'}, dimensions={0}, use_global_device_ids=true | all-gather | bytes 33280 | tf_op jit(solution)/shard_map/all_gather | solution.py:78
  61.4 0.2 slice_reduce_fusion
  61.6 0.2 slice_reduce_fusion.1
  61.9 0.1 constant_dynamic-slice_fusion.1
  61.9 0.1 pad_add_fusion.2
  62.0 0.1 compare_convert_fusion
  62.1 0.1 multiply_exponential_fusion.1
  62.2 0.1 and_convert_fusion
  62.3 0.1 multiply_exponential_fusion.2
  62.4 0.1 pad_add_fusion.1
  62.5 0.1 compare_convert_fusion.2
  62.5 0.4 copy.47
  63.0 0.6 maximum_convert_fusion
  63.6 2.3 %fusion.7 = f32[3,128,1024]{1,2,0:T(8,128)S(1)} fusion(f32[3,130,1024]{1,2,0:T(8,128)S(1)} %maximum_convert_fusion, f32[128]{0:T(128)S(1)} %get-tuple-element.36, f32[3,1024]{1,0:T(4,128)S(1)} %get-tuple-element.39, f32[128]{0:T(128)S(1)} %get-tuple-element.35, f32[3,1024]{1,0:T(4,128)S(1)} %get-tuple-element.40, f32[3,1024]{1,0:T(4,128)S(1)} %bitcast.47), kind=kLoop, calls=%fused_computation.13 | loop fusion | flops 2752512 | bytes 6329344 | tf_op jit(solution)/shard_map/add | solution.py:20
  65.9 0.8 fusion.10
  66.7 8.1 %all-to-all-start = ((bf16[128,64,16]{0,2,1:T(8,128)(2,1)}), bf16[128,64,16]{0,2,1:T(8,128)(2,1)S(1)}, u32[]{:S(2)}, u32[]{:S(2)}) async-start(bf16[128,64,16]{0,2,1:T(8,128)(2,1)} %bitcast.6), calls=%async_computation | async-start | bytes 524288 | tf_op jit(solution)/shard_map/all_to_all | solution.py:77
  74.9 0.1 broadcast_multiply_fusion.1
  75.0 0.2 multiply_exponential_fusion
  75.2 13.0 %all-to-all-done = bf16[128,64,16]{0,2,1:T(8,128)(2,1)S(1)} async-done(((bf16[128,64,16]{0,2,1:T(8,128)(2,1)}), bf16[128,64,16]{0,2,1:T(8,128)(2,1)S(1)}, u32[]{:S(2)}, u32[]{:S(2)}) %all-to-all-start) | async-done | bytes 262176 | tf_op jit(solution)/shard_map/all_to_all | solution.py:77
  88.3 0.6 bitcast_multiply_fusion
  88.9 6.1 %fusion = f32[64,128,128]{1,2,0:T(8,128)} fusion(f32[64,128,128]{1,2,0:T(8,128)S(1)} %bitcast_multiply_fusion, s32[64,128]{1,0:T(8,128)S(1)} %bitcast.46, pred[128,128]{1,0:T(8,128)(4,1)S(1)} %iota_compare_fusion), kind=kOutput, calls=%fused_computation.3 | convolution fusion | flops 1612709888 | bytes 8437760 | tf_op jit(solution)/shard_map/vmap()/dot_general | solution.py:33
  95.0 16.9 %copy.48 = f32[64,128,8,16]{3,2,1,0:T(8,128)} copy(f32[64,128,8,16]{1,3,2,0:T(8,128)} %bitcast.36) | data formatting | bytes 8388608 | tf_op jit(solution)/shard_map/vmap()/reshape | solution.py:33
  111.9 53.4 %multiply_reduce_fusion = (f32[64,128,16]{2,1,0:T(8,128)}, f32[64,128,8,16]{3,2,1,0:T(8,128)}) fusion(f32[8,16]{1,0:T(8,128)S(1)} %constant_dynamic-slice_fusion.1, f32[64,128,8,16]{3,2,1,0:T(8,128)} %copy.48, f32[128,8,16]{2,1,0:T(8,128)S(1)} %multiply_exponential_fusion), kind=kLoop, calls=%fused_computation | loop fusion | flops 3014656 | bytes 8978944 | tf_op jit(solution)/shard_map/vmap()/reduce_sum | solution.py:37
  165.3 1.0 slice_bitcast_fusion.1
  166.7 0.1 pad.44
  166.8 0.1 pad.45
  166.9 0.7 slice_bitcast_fusion.2
  167.6 0.1 pad.47
  167.7 0.1 pad.46
  167.9 2.8 %copy.49 = f32[64,128,16]{1,2,0:T(8,128)S(1)} copy(f32[64,128,16]{2,1,0:T(8,128)} %get-tuple-element.9) | data formatting | bytes 1048576 | tf_op jit(solution)/shard_map/vmap()/reduce_sum | solution.py:37
  170.7 0.2 pad.75
  171.0 0.2 pad.116
  171.3 0.6 multiply_reduce_fusion.2
  171.9 0.6 multiply_reduce_fusion.1
  172.6 0.1 multiply_add_fusion
  172.7 19.1 %all_to_all.26 = f32[64,128,16]{1,2,0:T(8,128)S(1)} all-to-all(f32[64,128,16]{1,2,0:T(8,128)S(1)} %multiply_add_fusion), channel_id=1, replica_groups=mesh['ctx'=64,'tp'=8] {'ctx'}, dimensions={0} | all-to-all | bytes 1048576 | tf_op jit(solution)/shard_map/all_to_all | solution.py:95
  191.8 0.2 fusion.12
  192.1 0.9 copy.50
  (52 shorter events, 0.6 us)
Async XLA Ops:
  0.0 61.8 %copy-start = (f32[8,1024]{1,0:T(8,128)S(1)}, f32[8,1024]{1,0:T(8,128)}, u32[]{:S(2)}) copy-start(f32[8,1024]{1,0:T(8,128)} %param.13) | copy-start | bytes 98308
  0.0 8.3 %copy-start.3 = (s32[128]{0:T(128)S(1)}, s32[128]{0:T(128)}, u32[]{:S(2)}) copy-start(s32[128]{0:T(128)} %param.15) | copy-start | bytes 1540
  0.0 61.8 %copy-start.2 = (f32[3,3,1024]{2,1,0:T(4,128)S(1)}, f32[3,3,1024]{2,1,0:T(4,128)}, u32[]{:S(2)}) copy-start(f32[3,3,1024]{2,1,0:T(4,128)} %param.11) | copy-start | bytes 110596
  4.0 58.5 %collective-permute-start = (bf16[3,2,1024]{2,1,0:T(2,128)(2,1)S(1)}, bf16[3,2,1024]{2,1,0:T(2,128)(2,1)S(1)}, u32[]{:S(2)}, u32[]{:S(2)}) collective-permute-start(bf16[3,2,1024]{2,1,0:T(2,128)(2,1)S(1)} %copy.46), channel_id=1, source_target_pairs={{0,8},{8,16},{16,24},{24,32},{32,40},{40,48},{48,56},{56,64},{64,7... | collective-permute-start | bytes 36872 | tf_op jit(solution)/shard_map/ppermute | solution.py:10
  8.4 54.0 %collective-permute-start.1 = (s32[2]{0:T(128)S(1)}, s32[2]{0:T(128)S(1)}, u32[]{:S(2)}, u32[]{:S(2)}) collective-permute-start(s32[2]{0:T(128)S(1)} %slice.217), channel_id=1, source_target_pairs={{0,8},{8,16},{16,24},{24,32},{32,40},{40,48},{48,56},{56,64},{64,7... | collective-permute-start | bytes 32 | tf_op jit(solution)/shard_map/ppermute | solution.py:10
  66.7 21.6 %all-to-all-start = ((bf16[128,64,16]{0,2,1:T(8,128)(2,1)}), bf16[128,64,16]{0,2,1:T(8,128)(2,1)S(1)}, u32[]{:S(2)}, u32[]{:S(2)}) async-start(bf16[128,64,16]{0,2,1:T(8,128)(2,1)} %bitcast.6), calls=%async_computation | async-start | bytes 524288 | tf_op jit(solution)/shard_map/all_to_all | solution.py:77
  171.9 19.9 %copy-start.4 = (f32[1024]{0:T(1024)S(1)}, f32[1024]{0:T(1024)}, u32[]{:S(2)}) copy-start(f32[1024]{0:T(1024)} %param.14) | copy-start | bytes 12292
  172.6 20.4 %copy-start.1 = (f32[8,1024]{1,0:T(8,128)S(1)}, f32[8,1024]{1,0:T(8,128)}, u32[]{:S(2)}) copy-start(f32[8,1024]{1,0:T(8,128)} %param.13) | copy-start | bytes 98308
where the time goes:
time: 194 us; the launch traced here: 193 us
  blocking collectives  67 us (35%)
  other arithmetic  61.6 us (32%)
  local copies, waits for them, and re-layouts  27.9 us (14%)
  starting transfers between devices  16.7 us (9%)
  waiting for transfers between devices  13 us (7%)
  matrix products  6.12 us (3%)
    reduce_sum x1, other arithmetic, mode_terms_all(): long_part = jnp.sum(residues[None] * states, axis=1)  53.4 us
    all_gather x1, blocking collectives, on_device(): ids_all = lax.all_gather(doc_ids, 'ctx', axis=0, tiled=True)  47.9 us
    all_to_all x1, blocking collectives, on_device(): lax.all_to_all(grouped, 'ctx', split_axis=0, concat_axis=1, tiled=True)  19.1 us
    reshape x1, local copies, waits for them, and re-layouts, mode_terms_all(): jnp.dot(mask, weighted, precision=lax.Precision.HIGHEST)  16.9 us
    all_to_all x1, waiting for transfers between devices, on_device(): lax.all_to_all(gated, 'ctx', split_axis=1, concat_axis=0, tiled=True)  13 us
    ppermute x2, starting transfers between devices, shifted_2(): lax.ppermute(value, axis, [(source, source + steps) for source in range(f...  8.54 us
    all_to_all x1, starting transfers between devices, on_device(): lax.all_to_all(gated, 'ctx', split_axis=1, concat_axis=0, tiled=True)  8.13 us
    dot_general x1, matrix products, mode_terms_all(): jnp.dot(mask, weighted, precision=lax.Precision.HIGHEST)  6.12 us
  transfers between devices with their start and end apart: 3, of which 1 were waited for; matrix products, arithmetic and copies ran while one was open for 1% of the time, Pallas kernels for 0%

commit v1 on v0

--- a/solution.py
+++ b/solution.py
@@ -75,7 +75,9 @@
     n_ctx = lax.axis_size("ctx")
     group_width = channels // n_ctx
     whole = lax.all_to_all(gated, "ctx", split_axis=1, concat_axis=0, tiled=True)
-    ids_all = lax.all_gather(doc_ids, "ctx", axis=0, tiled=True)
+    ids_all = jnp.concatenate(
+        lax.all_to_all(jnp.stack([doc_ids] * lax.axis_size("ctx")), "ctx", 0, 0), axis=0
+    )
     offset = lax.axis_index("ctx") * group_width
     rate_sub = lax.dynamic_slice_in_dim(rates, offset, group_width, 1)
     resid_sub = lax.dynamic_slice_in_dim(residues, offset, group_width, 1)

time: 194 us -> 168 us (0.87)
  the two profiles are of different devices: /device:TPU:4 before, /device:TPU:2 now
where the time goes in v1:
time: 168 us; the launch traced here: 167 us
  other arithmetic  61.6 us (37%)
  starting transfers between devices  30 us (18%)
  local copies, waits for them, and re-layouts  28.5 us (17%)
  blocking collectives  21.4 us (13%)
  waiting for transfers between devices  19.2 us (11%)
  matrix products  6.11 us (4%)
    reduce_sum x1, other arithmetic, mode_terms_all(): long_part = jnp.sum(residues[None] * states, axis=1)  53.4 us
    all_to_all x1, blocking collectives, on_device(): lax.all_to_all(grouped, 'ctx', split_axis=0, concat_axis=1, tiled=True)  21.4 us
    reshape x1, local copies, waits for them, and re-layouts, mode_terms_all(): jnp.dot(mask, weighted, precision=lax.Precision.HIGHEST)  16.9 us
    all_to_all x1, starting transfers between devices, on_device(): lax.all_to_all(jnp.stack([doc_ids] * lax.axis_size('ctx')), 'ctx', 0, 0)  14.8 us
    all_to_all x1, waiting for transfers between devices, on_device(): lax.all_to_all(gated, 'ctx', split_axis=1, concat_axis=0, tiled=True)  13.1 us
    ppermute x2, starting transfers between devices, shifted_2(): lax.ppermute(value, axis, [(source, source + steps) for source in range(f...  8.54 us
    all_to_all x1, starting transfers between devices, on_device(): lax.all_to_all(gated, 'ctx', split_axis=1, concat_axis=0, tiled=True)  6.72 us
    all_to_all x1, waiting for transfers between devices, on_device(): lax.all_to_all(jnp.stack([doc_ids] * lax.axis_size('ctx')), 'ctx', 0, 0)  6.16 us
  transfers between devices with their start and end apart: 4, of which 2 were waited for; matrix products, arithmetic and copies ran while one was open for 4% of the time, Pallas kernels for 0%

profile of v1, /device:TPU:2, one launch (start us, length us, event | category | flops | bytes accessed | tf_op | source)
XLA Modules:
  0.0 167.5 jit_solution(15131963026310935058)
XLA Ops:
  0.0 1.1 copy.57
  1.2 1.1 copy.56
  2.3 1.1 copy.55
  3.4 0.3 pad_maximum_fusion
  3.7 0.3 copy.58
  4.0 4.3 %collective-permute-start = (bf16[3,2,1024]{2,1,0:T(2,128)(2,1)S(1)}, bf16[3,2,1024]{2,1,0:T(2,128)(2,1)S(1)}, u32[]{:S(2)}, u32[]{:S(2)}) collective-permute-start(bf16[3,2,1024]{2,1,0:T(2,128)(2,1)S(1)} %copy.58), channel_id=1, source_target_pairs={{0,8},{8,16},{16,24},{24,32},{32,40},{40,48},{48,56},{56,64},{64,7... | collective-permute-start | bytes 36872 | tf_op jit(solution)/shard_map/ppermute | solution.py:10
  8.3 0.1 slice.217
  8.4 4.3 %collective-permute-start.1 = (s32[2]{0:T(128)S(1)}, s32[2]{0:T(128)S(1)}, u32[]{:S(2)}, u32[]{:S(2)}) collective-permute-start(s32[2]{0:T(128)S(1)} %slice.217), channel_id=1, source_target_pairs={{0,8},{8,16},{16,24},{24,32},{32,40},{40,48},{48,56},{56,64},{64,7... | collective-permute-start | bytes 32 | tf_op jit(solution)/shard_map/ppermute | solution.py:10
  12.7 0.6 stack.14
  13.3 14.8 %all-to-all-start = ((s32[64,1,128]{2,1,0:T(1,128)}), s32[64,1,128]{2,1,0:T(1,128)S(1)}, u32[]{:S(2)}, u32[]{:S(2)}) async-start(s32[64,1,128]{2,1,0:T(1,128)} %stack.14), calls=%async_computation | async-start | bytes 65536 | tf_op jit(solution)/shard_map/all_to_all | solution.py:79
  28.1 0.8 multiply_exponential_fusion.4
  28.9 0.1 mul.302
  29.1 0.1 constant_dynamic-slice_fusion.1
  29.1 0.1 multiply_exponential_fusion.1
  29.2 0.2 multiply_exponential_fusion
  29.5 0.1 multiply_exponential_fusion.2
  29.6 0.1 pad_add_fusion.1
  29.7 0.1 compare_convert_fusion.2
  29.8 0.4 copy.59
  30.2 0.6 maximum_convert_fusion
  30.8 2.3 %fusion.7 = f32[3,128,1024]{1,2,0:T(8,128)S(1)} fusion(f32[3,130,1024]{1,2,0:T(8,128)S(1)} %maximum_convert_fusion, f32[128]{0:T(128)S(1)} %get-tuple-element.36, f32[3,1024]{1,0:T(4,128)S(1)} %get-tuple-element.39, f32[128]{0:T(128)S(1)} %get-tuple-element.35, f32[3,1024]{1,0:T(4,128)S(1)} %get-tuple-element.40, f32[3,1024]{1,0:T(4,128)S(1)} %bitcast.46), kind=kLoop, calls=%fused_computation.13 | loop fusion | flops 2752512 | bytes 6329344 | tf_op jit(solution)/shard_map/add | solution.py:20
  33.1 0.8 fusion.10
  33.9 6.2 %all-to-all-done = s32[64,1,128]{2,1,0:T(1,128)S(1)} async-done(((s32[64,1,128]{2,1,0:T(1,128)}), s32[64,1,128]{2,1,0:T(1,128)S(1)}, u32[]{:S(2)}, u32[]{:S(2)}) %all-to-all-start) | async-done | bytes 32800 | tf_op jit(solution)/shard_map/all_to_all | solution.py:79
  40.0 6.7 %all-to-all-start.1 = ((bf16[128,64,16]{0,2,1:T(8,128)(2,1)}), bf16[128,64,16]{0,2,1:T(8,128)(2,1)S(1)}, u32[]{:S(2)}, u32[]{:S(2)}) async-start(bf16[128,64,16]{0,2,1:T(8,128)(2,1)} %bitcast.5), calls=%async_computation.1 | async-start | bytes 524288 | tf_op jit(solution)/shard_map/all_to_all | solution.py:77
  46.8 0.2 slice_reduce_fusion
  47.0 0.2 slice_reduce_fusion.1
  47.1 0.1 and_convert_fusion
  47.2 0.1 pad_add_fusion.2
  47.3 0.1 compare_convert_fusion
  47.4 0.1 broadcast_multiply_fusion.1
  47.5 13.1 %all-to-all-done.1 = bf16[128,64,16]{0,2,1:T(8,128)(2,1)S(1)} async-done(((bf16[128,64,16]{0,2,1:T(8,128)(2,1)}), bf16[128,64,16]{0,2,1:T(8,128)(2,1)S(1)}, u32[]{:S(2)}, u32[]{:S(2)}) %all-to-all-start.1) | async-done | bytes 262176 | tf_op jit(solution)/shard_map/all_to_all | solution.py:77
  60.6 0.6 bitcast_multiply_fusion
  61.2 6.1 %fusion = f32[64,128,128]{1,2,0:T(8,128)} fusion(f32[64,128,128]{1,2,0:T(8,128)S(1)} %bitcast_multiply_fusion, s32[64,128]{1,0:T(8,128)S(1)} %bitcast.45, pred[128,128]{1,0:T(8,128)(4,1)S(1)} %iota_compare_fusion), kind=kOutput, calls=%fused_computation.3 | convolution fusion | flops 1612709888 | bytes 8437760 | tf_op jit(solution)/shard_map/vmap()/dot_general | solution.py:33
  67.3 16.9 %copy.60 = f32[64,128,8,16]{3,2,1,0:T(8,128)} copy(f32[64,128,8,16]{1,3,2,0:T(8,128)} %bitcast.35) | data formatting | bytes 8388608 | tf_op jit(solution)/shard_map/vmap()/reshape | solution.py:33
  84.2 53.4 %multiply_reduce_fusion = (f32[64,128,16]{2,1,0:T(8,128)}, f32[64,128,8,16]{3,2,1,0:T(8,128)}) fusion(f32[8,16]{1,0:T(8,128)S(1)} %constant_dynamic-slice_fusion.1, f32[64,128,8,16]{3,2,1,0:T(8,128)} %copy.60, f32[128,8,16]{2,1,0:T(8,128)S(1)} %multiply_exponential_fusion), kind=kLoop, calls=%fused_computation | loop fusion | flops 3014656 | bytes 8978944 | tf_op jit(solution)/shard_map/vmap()/reduce_sum | solution.py:37
  137.6 1.0 slice_bitcast_fusion.1
  139.2 0.7 slice_bitcast_fusion.2
  139.9 0.1 pad.47
  140.0 0.1 pad.46
  140.2 2.8 %copy.61 = f32[64,128,16]{1,2,0:T(8,128)S(1)} copy(f32[64,128,16]{2,1,0:T(8,128)} %get-tuple-element.9) | data formatting | bytes 1048576 | tf_op jit(solution)/shard_map/vmap()/reduce_sum | solution.py:37
  143.0 0.2 pad.75
  143.3 0.2 pad.116
  143.6 0.6 multiply_reduce_fusion.2
  144.2 0.6 multiply_reduce_fusion.1
  144.9 0.1 multiply_add_fusion
  145.0 21.4 %all_to_all.32 = f32[64,128,16]{1,2,0:T(8,128)S(1)} all-to-all(f32[64,128,16]{1,2,0:T(8,128)S(1)} %multiply_add_fusion), channel_id=1, replica_groups=mesh['ctx'=64,'tp'=8] {'ctx'}, dimensions={0} | all-to-all | bytes 1048576 | tf_op jit(solution)/shard_map/all_to_all | solution.py:97
  166.4 0.2 fusion.12
  166.6 0.9 copy.62
  (54 shorter events, 0.7 us)
Async XLA Ops:
  0.0 29.1 %copy-start = (f32[8,1024]{1,0:T(8,128)S(1)}, f32[8,1024]{1,0:T(8,128)}, u32[]{:S(2)}) copy-start(f32[8,1024]{1,0:T(8,128)} %param.13) | copy-start | bytes 98308
  0.0 8.3 %copy-start.3 = (s32[128]{0:T(128)S(1)}, s32[128]{0:T(128)}, u32[]{:S(2)}) copy-start(s32[128]{0:T(128)} %param.15) | copy-start | bytes 1540
  0.0 29.0 %copy-start.2 = (f32[3,3,1024]{2,1,0:T(4,128)S(1)}, f32[3,3,1024]{2,1,0:T(4,128)}, u32[]{:S(2)}) copy-start(f32[3,3,1024]{2,1,0:T(4,128)} %param.11) | copy-start | bytes 110596
  4.0 25.7 %collective-permute-start = (bf16[3,2,1024]{2,1,0:T(2,128)(2,1)S(1)}, bf16[3,2,1024]{2,1,0:T(2,128)(2,1)S(1)}, u32[]{:S(2)}, u32[]{:S(2)}) collective-permute-start(bf16[3,2,1024]{2,1,0:T(2,128)(2,1)S(1)} %copy.58), channel_id=1, source_target_pairs={{0,8},{8,16},{16,24},{24,32},{32,40},{40,48},{48,56},{56,64},{64,7... | collective-permute-start | bytes 36872 | tf_op jit(solution)/shard_map/ppermute | solution.py:10
  8.4 21.2 %collective-permute-start.1 = (s32[2]{0:T(128)S(1)}, s32[2]{0:T(128)S(1)}, u32[]{:S(2)}, u32[]{:S(2)}) collective-permute-start(s32[2]{0:T(128)S(1)} %slice.217), channel_id=1, source_target_pairs={{0,8},{8,16},{16,24},{24,32},{32,40},{40,48},{48,56},{56,64},{64,7... | collective-permute-start | bytes 32 | tf_op jit(solution)/shard_map/ppermute | solution.py:10
  13.3 26.8 %all-to-all-start = ((s32[64,1,128]{2,1,0:T(1,128)}), s32[64,1,128]{2,1,0:T(1,128)S(1)}, u32[]{:S(2)}, u32[]{:S(2)}) async-start(s32[64,1,128]{2,1,0:T(1,128)} %stack.14), calls=%async_computation | async-start | bytes 65536 | tf_op jit(solution)/shard_map/all_to_all | solution.py:79
  40.0 20.5 %all-to-all-start.1 = ((bf16[128,64,16]{0,2,1:T(8,128)(2,1)}), bf16[128,64,16]{0,2,1:T(8,128)(2,1)S(1)}, u32[]{:S(2)}, u32[]{:S(2)}) async-start(bf16[128,64,16]{0,2,1:T(8,128)(2,1)} %bitcast.5), calls=%async_computation.1 | async-start | bytes 524288 | tf_op jit(solution)/shard_map/all_to_all | solution.py:77
  144.2 22.2 %copy-start.4 = (f32[1024]{0:T(1024)S(1)}, f32[1024]{0:T(1024)}, u32[]{:S(2)}) copy-start(f32[1024]{0:T(1024)} %param.14) | copy-start | bytes 12292
  144.9 22.6 %copy-start.1 = (f32[8,1024]{1,0:T(8,128)S(1)}, f32[8,1024]{1,0:T(8,128)}, u32[]{:S(2)}) copy-start(f32[8,1024]{1,0:T(8,128)} %param.13) | copy-start | bytes 98308
